TPU v7x, 32 devices: a whole 2x2x4 slice. The times are simulated.
32 devices in a mesh: wide: 8 (over y, x, core), narrow: 4 (over z).
Axes of the slice: x: 2, y: 2, z: 4, core: 2. Of those that a mesh axis runs over, the one named last changes fastest.
Arguments:
- activity: bfloat16 [32, 8, 512, 512], P(('wide', 'narrow')), may hold values from 0 to 1
- tile_coords: int32 [32, 2], replicated, may hold values from 0 to 7, as said below
- user_owner: int32 [8], replicated, may hold values from 0 to 7, each once
- item_owner: int32 [8], replicated, may hold values from 0 to 7, each once
- user_factor: float32 [4096, 256], P('wide', 'narrow'), may hold values from 0 to 1
- item_factor: float32 [4096, 256], P('wide', 'narrow'), may hold values from 0 to 1
- time_factor: float32 [8, 256], replicated, may hold values from 0.0003 to 0.003
- user_dual: float32 [4096, 256], P('wide', 'narrow'), may hold values from -1.8 to 1.8
- item_dual: float32 [4096, 256], P('wide', 'narrow'), may hold values from -1.8 to 1.8
Outputs:
- new_users: float32 [4096, 256], P('wide', 'narrow')
- new_items: float32 [4096, 256], P('wide', 'narrow')
- new_user_dual: float32 [4096, 256], P('wide', 'narrow')
- new_item_dual: float32 [4096, 256], P('wide', 'narrow')
Inputs may be any that keep to these rules, and one draw needn't show every extreme that they name: `tile_coords`: no pair of blocks appears twice. `user_owner`: each stored row block holds exactly one user block. `item_owner`: each stored row block holds exactly one item block.
All inputs are finite; a program needn't handle non-finite values.
Results may differ from a plain program's by a relative error of at most 0.0017.
The roundings to bfloat16 on the way count: a program that leaves them out, or rounds other values in their place, can miss the bound.
Values may be sent and summed in bfloat16 or wider, within the bound.
No kernel may reach another device: no remote copies, remote signals or barrier semaphores. Data moves between devices by JAX's collectives and lax.ppermute only.
A program may use at most 64 MiB of HBM per device.

v0:
```python
import jax
import jax.numpy as jnp
from jax import lax
from jax.sharding import PartitionSpec as P

RANK = 256
BLOCK = 512
PASSES = 2


def locate(owner, wanted_blocks):
    everyone = jnp.arange(owner.shape[0], dtype=jnp.int32)
    chosen = jnp.where(everyone[None, :] == wanted_blocks[:, None], owner[None, :], 0)
    return jnp.sum(chosen, axis=1)


def fetch_rows(factor, wanted):
    lowered = factor.astype(jnp.bfloat16)
    width = factor.shape[1]
    slots = wanted.shape[0]
    initial = jnp.zeros((slots, BLOCK, width), jnp.bfloat16)
    portion = lax.all_gather(lowered, "wide", axis=0, tiled=True)
    count_blocks = portion.shape[0] // BLOCK
    shaped = portion.reshape(count_blocks, BLOCK, width)
    first = jnp.int32(0) // BLOCK
    onehot = (wanted[:, None] == first + jnp.arange(count_blocks, dtype=jnp.int32)[None, :]).astype(
        jnp.bfloat16
    )
    picked = jnp.einsum("jq,qrc->jrc", onehot, shaped, preferred_element_type=jnp.float32)
    gathered = initial + picked.astype(jnp.bfloat16)
    return lax.all_to_all(gathered, "narrow", split_axis=0, concat_axis=2, tiled=True)


def tile_sums(activity, fetched, time_factor, forward):
    khatri = (fetched.astype(jnp.float32)[:, None] * time_factor[None, :, None, :]).astype(
        jnp.bfloat16
    )
    if forward:
        return jnp.einsum("tkij,tkjr->tir", activity, khatri, preferred_element_type=jnp.float32)
    return jnp.einsum("tkij,tkir->tjr", activity, khatri, preferred_element_type=jnp.float32)


def owner_sums(partial_value, targets, owned):
    received = lax.all_to_all(partial_value, "narrow", split_axis=2, concat_axis=0, tiled=True)
    width = received.shape[2]
    count_blocks = owned * lax.axis_size("wide") // BLOCK
    onehot = (jnp.arange(count_blocks, dtype=jnp.int32)[:, None] == targets[None, :]).astype(
        jnp.float32
    )
    placed = jnp.einsum("qj,jrc->qrc", onehot, received, precision=lax.Precision.HIGHEST)
    return lax.psum_scatter(
        placed.reshape(owned * lax.axis_size("wide"), width),
        "wide",
        scatter_dimension=0,
        tiled=True,
    )


def joint_gram(other_rows, time_factor):
    local_gram = jnp.dot(other_rows.T, other_rows, precision=lax.Precision.HIGHEST)
    total = lax.psum(local_gram, ("wide", "narrow"))
    gram = total * jnp.dot(time_factor.T, time_factor, precision=lax.Precision.HIGHEST)
    penalty = jnp.trace(gram) / RANK
    identity = jnp.eye(RANK, dtype=jnp.float32)
    lower = jnp.linalg.cholesky(gram + penalty * identity)
    inverse = jax.scipy.linalg.cho_solve((lower, True), identity)
    return (penalty, inverse)


def update_rows(
    activity, other_cols, other_rows, factor, dual, wanted, targets, time_factor, forward, owned
):
    fetched = fetch_rows(other_cols, wanted)
    partial_value = tile_sums(activity, fetched, time_factor, forward)
    sums = owner_sums(partial_value, targets, owned)
    sums_rows = lax.all_to_all(sums, "narrow", split_axis=0, concat_axis=1, tiled=True)
    penalty, inverse = joint_gram(other_rows, time_factor)
    for _ in range(PASSES):
        target = jnp.dot(
            sums_rows + penalty * (factor + dual), inverse, precision=lax.Precision.HIGHEST
        )
        factor = jnp.maximum(target - dual, 0.0)
        dual = dual + factor - target
    factor_cols, dual_cols = (
        lax.all_to_all(factor, "narrow", split_axis=1, concat_axis=0, tiled=True),
        lax.all_to_all(dual, "narrow", split_axis=1, concat_axis=0, tiled=True),
    )
    return (factor_cols, dual_cols, factor)


def local(
    activity,
    tile_coords,
    user_owner,
    item_owner,
    user_factor,
    item_factor,
    time_factor,
    user_dual,
    item_dual,
):
    narrow_size = lax.axis_size("narrow")
    slots = narrow_size * activity.shape[0]
    group_coords = lax.dynamic_slice_in_dim(tile_coords, lax.axis_index("wide") * slots, slots, 0)
    user_pos = locate(user_owner, group_coords[:, 0])
    item_pos = locate(item_owner, group_coords[:, 1])
    owned = user_factor.shape[0]
    user_rows, udual_rows, item_rows, idual_rows = (
        lax.all_to_all(user_factor, "narrow", split_axis=0, concat_axis=1, tiled=True),
        lax.all_to_all(user_dual, "narrow", split_axis=0, concat_axis=1, tiled=True),
        lax.all_to_all(item_factor, "narrow", split_axis=0, concat_axis=1, tiled=True),
        lax.all_to_all(item_dual, "narrow", split_axis=0, concat_axis=1, tiled=True),
    )
    new_users, new_user_dual, fresh_rows = update_rows(
        activity,
        item_factor,
        item_rows,
        user_rows,
        udual_rows,
        item_pos,
        user_pos,
        time_factor,
        True,
        owned,
    )
    new_items, new_item_dual, _ = update_rows(
        activity,
        new_users,
        fresh_rows,
        item_rows,
        idual_rows,
        user_pos,
        item_pos,
        time_factor,
        False,
        owned,
    )
    return (new_users, new_items, new_user_dual, new_item_dual)


def solution(mesh):
    in_specs = (
        P(("wide", "narrow"), None, None, None),
        P(),
        P(),
        P(),
        P("wide", "narrow"),
        P("wide", "narrow"),
        P(),
        P("wide", "narrow"),
        P("wide", "narrow"),
    )
    out_specs = (P("wide", "narrow"), P("wide", "narrow"), P("wide", "narrow"), P("wide", "narrow"))
    return jax.shard_map(local, mesh=mesh, in_specs=in_specs, out_specs=out_specs, check_vma=False)
```

profile of v0, /device:TPU:0, one launch (start us, length us, event | category | flops | bytes accessed | tf_op | source)
XLA Modules:
  0.0 562.6 jit_solution(15027327676209226072)
XLA Ops:
  8.0 1.6 copy_bitcast_fusion.8
  9.6 6.3 %all-to-all-start.3 = ((f32[4,128,64]{1,2,0:T(8,128)}), f32[4,128,64]{1,2,0:T(8,128)S(1)}, u32[]{:S(2)}, u32[]{:S(2)}) async-start(f32[4,128,64]{1,2,0:T(8,128)} %copy_bitcast_fusion.8), calls=%async_computation.4 | async-start | bytes 262144 | tf_op jit(solution)/shard_map/all_to_all | solution.py:111
  16.0 0.9 convert_element_type.70
  16.9 9.9 %all_gather.6 = bf16[4096,64]{0,1:T(8,128)(2,1)S(1)} all-gather(bf16[512,64]{0,1:T(8,128)(2,1)S(1)} %convert_element_type.70), channel_id=1, replica_groups=mesh['wide'=8,'narrow'=4] {'wide'}, dimensions={0}, use_global_device_ids=true | all-gather | bytes 589824 | tf_op jit(solution)/shard_map/all_gather | solution.py:22
  28.4 1.6 copy_bitcast_fusion.6
  29.9 0.8 select_reduce_fusion.6
  31.1 0.8 select_reduce_fusion.7
  32.0 1.6 copy_bitcast_fusion.4
  33.5 5.1 all-to-all-start.4
  38.6 1.1 fusion.86
  39.7 5.3 all-to-all-done.4
  45.1 3.3 all-to-all-start.5
  49.3 5.1 all-to-all-done.5
  54.3 3.4 all-to-all-start
  57.8 116.1 %all-reduce.4.cloned.1.call-done = f32[256,256]{0,1:T(8,128)} async-done(((f32[256,256]{0,1:T(8,128)}), f32[256,256]{0,1:T(8,128)}) %all-reduce.4.cloned.1.call-update) | async-done | bytes 262160 | tf_op jit(solution)/shard_map/psum | solution.py:61
  173.9 2.0 select_reduce_fusion.1
  176.8 11.7 %cholesky.130 = f32[128,128]{1,0:T(8,128)S(1)} custom-call(f32[128,128]{1,0:T(8,128)S(1)} %cholesky.194), custom_call_target="Cholesky" | custom-call | tf_op jit(solution)/shard_map/jit(cholesky)/cholesky | solution.py:65
  188.6 9.8 %custom-call.15 = f32[1,128,128]{1,2,0:T(8,128)S(1)} custom-call(f32[1,128,128]{2,1,0:T(8,128)S(1)} %get-tuple-element.59), custom_call_target="InvertDiagBlocksLowerTriangular" | custom-call | tf_op jit(solution)/shard_map/jit(cholesky)/cholesky | solution.py:65
  198.7 3.5 fusion.8
  202.1 1.3 copy.174
  203.5 3.6 all-to-all-start.1
  207.8 11.7 %cholesky.147 = f32[128,128]{1,0:T(8,128)S(1)} custom-call(f32[128,128]{1,0:T(8,128)S(1)} %convolution_subtract_fusion.5), custom_call_target="Cholesky" | custom-call | tf_op jit(solution)/shard_map/jit(cholesky)/cholesky | solution.py:65
  221.6 1.0 fusion.16
  222.6 1.6 copy.231
  224.3 4.0 while.4
  224.9 1.4 bitcast_dynamic-update-slice_fusion.4
  226.9 1.4 bitcast_dynamic-update-slice_fusion.4
  228.3 19.7 %custom-call.16 = f32[2,128,128]{1,2,0:T(8,128)S(1)} custom-call(f32[2,128,128]{2,1,0:T(8,128)S(1)} %get-tuple-element.20), custom_call_target="InvertDiagBlocksLowerTriangular" | custom-call | tf_op jit(solution)/shard_map/jit(_cho_solve)/triangular_solve | solution.py:66
  249.6 12.0 %reduce-scatter.3.cloned.1.call-done = f32[512,64]{0,1:T(8,128)} async-done(((f32[4096,64]{0,1:T(8,128)}), f32[512,64]{0,1:T(8,128)}) %reduce-scatter.3.cloned.1.call-update) | async-done | bytes 131088 | tf_op jit(solution)/shard_map/reduce_scatter | solution.py:51
  261.6 1.6 copy_bitcast_fusion.9
  263.2 4.6 all-to-all-start.2
  268.1 5.7 %all-to-all-done.2 = f32[4,128,64]{1,2,0:T(8,128)S(1)} async-done(((f32[4,128,64]{1,2,0:T(8,128)}), f32[4,128,64]{1,2,0:T(8,128)S(1)}, u32[]{:S(2)}, u32[]{:S(2)}) %all-to-all-start.2) | async-done | bytes 131104 | tf_op jit(solution)/shard_map/all_to_all | solution.py:76
  273.7 3.3 all-to-all-start.10
  277.8 1.1 fusion.87
  279.1 3.9 all-to-all-done.10
  283.0 0.8 copy.190
  283.8 3.3 all-to-all-start.6
  287.9 122.6 %all-reduce.6.cloned.1.call-done = f32[256,256]{0,1:T(8,128)} async-done(((f32[256,256]{0,1:T(8,128)}), f32[256,256]{0,1:T(8,128)}) %all-reduce.6.cloned.1.call-update) | async-done | bytes 262160 | tf_op jit(solution)/shard_map/psum | solution.py:61
  410.5 1.6 select_reduce_fusion
  413.6 10.0 %all_gather.7 = bf16[4096,64]{0,1:T(8,128)(2,1)S(1)} all-gather(bf16[512,64]{0,1:T(8,128)(2,1)S(1)} %get-tuple-element.40), channel_id=1, replica_groups=mesh['wide'=8,'narrow'=4] {'wide'}, dimensions={0}, use_global_device_ids=true | all-gather | bytes 589824 | tf_op jit(solution)/shard_map/all_gather | solution.py:22
  424.9 3.6 all-to-all-start.7
  428.5 11.7 %cholesky.164 = f32[128,128]{1,0:T(8,128)S(1)} custom-call(f32[128,128]{1,0:T(8,128)S(1)} %cholesky.197), custom_call_target="Cholesky" | custom-call | tf_op jit(solution)/shard_map/jit(cholesky)/cholesky | solution.py:65
  440.3 9.8 %custom-call.17 = f32[1,128,128]{1,2,0:T(8,128)S(1)} custom-call(f32[1,128,128]{2,1,0:T(8,128)S(1)} %get-tuple-element.55), custom_call_target="InvertDiagBlocksLowerTriangular" | custom-call | tf_op jit(solution)/shard_map/jit(cholesky)/cholesky | solution.py:65
  450.4 3.5 fusion.11
  453.9 1.3 copy.193
  455.2 5.1 all-to-all-start.8
  460.8 11.7 %cholesky.181 = f32[128,128]{1,0:T(8,128)S(1)} custom-call(f32[128,128]{1,0:T(8,128)S(1)} %convolution_subtract_fusion.4), custom_call_target="Cholesky" | custom-call | tf_op jit(solution)/shard_map/jit(cholesky)/cholesky | solution.py:65
  475.2 1.0 fusion.14
  476.3 1.6 copy.233
  477.9 4.0 while.5
  478.5 1.4 bitcast_dynamic-update-slice_fusion.5
  480.5 1.4 bitcast_dynamic-update-slice_fusion.5
  481.9 19.7 %custom-call.18 = f32[2,128,128]{1,2,0:T(8,128)S(1)} custom-call(f32[2,128,128]{2,1,0:T(8,128)S(1)} %get-tuple-element.21), custom_call_target="InvertDiagBlocksLowerTriangular" | custom-call | tf_op jit(solution)/shard_map/jit(_cho_solve)/triangular_solve | solution.py:66
  503.2 11.4 %reduce-scatter.5.cloned.1.call-done = f32[512,64]{0,1:T(8,128)} async-done(((f32[4096,64]{0,1:T(8,128)}), f32[512,64]{0,1:T(8,128)}) %reduce-scatter.5.cloned.1.call-update) | async-done | bytes 131088 | tf_op jit(solution)/shard_map/reduce_scatter | solution.py:51
  514.6 1.6 copy_bitcast_fusion.5
  516.1 4.6 all-to-all-start.9
  521.0 5.7 %all-to-all-done.9 = f32[4,128,64]{1,2,0:T(8,128)S(1)} async-done(((f32[4,128,64]{1,2,0:T(8,128)}), f32[4,128,64]{1,2,0:T(8,128)S(1)}, u32[]{:S(2)}, u32[]{:S(2)}) %all-to-all-start.9) | async-done | bytes 131104 | tf_op jit(solution)/shard_map/all_to_all | solution.py:76
  526.6 3.3 all-to-all-start.12
  530.7 0.8 copy.207
  531.4 4.4 all-to-all-done.12
  535.9 3.3 all-to-all-start.11
  540.6 4.5 all-to-all-done.11
  545.1 3.3 all-to-all-start.13
  549.1 5.2 all-to-all-done.13
  (95 shorter events, 20.5 us)
Async XLA Ops:
  8.0 19.7 %copy-start = (f32[512,64]{0,1:T(8,128)S(1)}, f32[512,64]{0,1:T(8,128)}, u32[]{:S(2)}) copy-start(f32[512,64]{0,1:T(8,128)} %param.16) | copy-start | bytes 393220
  8.0 165.9 %copy-start.1 = (f32[8,256]{1,0:T(8,128)S(1)}, f32[8,256]{1,0:T(8,128)}, u32[]{:S(2)}) copy-start(f32[8,256]{1,0:T(8,128)} %param.18) | copy-start | bytes 24580
  9.6 23.9 %all-to-all-start.3 = ((f32[4,128,64]{1,2,0:T(8,128)}), f32[4,128,64]{1,2,0:T(8,128)S(1)}, u32[]{:S(2)}, u32[]{:S(2)}) async-start(f32[4,128,64]{1,2,0:T(8,128)} %copy_bitcast_fusion.8), calls=%async_computation.4 | async-start | bytes 262144 | tf_op jit(solution)/shard_map/all_to_all | solution.py:111
  33.5 11.5 %all-to-all-start.4 = ((f32[4,128,64]{1,2,0:T(8,128)}), f32[4,128,64]{1,2,0:T(8,128)S(1)}, u32[]{:S(2)}, u32[]{:S(2)}) async-start(f32[4,128,64]{1,2,0:T(8,128)} %copy_bitcast_fusion.7), calls=%async_computation.5 | async-start | bytes 262144 | tf_op jit(solution)/shard_map/all_to_all | solution.py:109
  38.6 135.3 %all-reduce.4.cloned.1.call-start = ((), (), s32[]{:S(2)}) async-start(), calls=%async_computation.17 | async-start | bytes 524288 | tf_op jit(solution)/shard_map/psum | solution.py:61
  45.1 9.3 %all-to-all-start.5 = ((f32[4,128,64]{1,2,0:T(8,128)}), f32[4,128,64]{1,2,0:T(8,128)S(1)}, u32[]{:S(2)}, u32[]{:S(2)}) async-start(f32[4,128,64]{1,2,0:T(8,128)} %copy_bitcast_fusion.6), calls=%async_computation.6 | async-start | bytes 262144 | tf_op jit(solution)/shard_map/all_to_all | solution.py:110
  54.3 144.3 %all-to-all-start = ((bf16[4,512,64]{1,2,0:T(8,128)(2,1)}), bf16[4,512,64]{1,2,0:T(8,128)(2,1)S(1)}, u32[]{:S(2)}, u32[]{:S(2)}) async-start(bf16[4,512,64]{1,2,0:T(8,128)(2,1)} %copy.173), calls=%async_computation | async-start | bytes 524288 | tf_op jit(solution)/shard_map/all_to_all | solution.py:31
  203.5 18.1 %all-to-all-start.1 = ((f32[1,512,256]{1,0,2:T(1,128)}), f32[1,512,256]{1,0,2:T(1,128)S(1)}, u32[]{:S(2)}, u32[]{:S(2)}) async-start(f32[1,512,256]{1,0,2:T(1,128)} %copy.174), calls=%async_computation.1 | async-start | bytes 1048576 | tf_op jit(solution)/shard_map/all_to_all | solution.py:44
  207.1 54.6 %reduce-scatter.3.cloned.1.call-start = ((), (), s32[]{:S(2)}) async-start(), calls=%async_computation.16 | async-start | bytes 1179648 | tf_op jit(solution)/shard_map/reduce_scatter | solution.py:51
  263.2 10.5 %all-to-all-start.2 = ((f32[4,128,64]{1,2,0:T(8,128)}), f32[4,128,64]{1,2,0:T(8,128)S(1)}, u32[]{:S(2)}, u32[]{:S(2)}) async-start(f32[4,128,64]{1,2,0:T(8,128)} %copy_bitcast_fusion.9), calls=%async_computation.3 | async-start | bytes 262144 | tf_op jit(solution)/shard_map/all_to_all | solution.py:76
  273.7 9.2 %all-to-all-start.10 = ((f32[4,128,64]{1,2,0:T(8,128)}), f32[4,128,64]{1,2,0:T(8,128)S(1)}, u32[]{:S(2)}, u32[]{:S(2)}) async-start(f32[4,128,64]{1,2,0:T(8,128)} %copy_bitcast_fusion.4), calls=%async_computation.12 | async-start | bytes 262144 | tf_op jit(solution)/shard_map/all_to_all | solution.py:112
  277.1 133.4 %all-reduce.6.cloned.1.call-start = ((), (), s32[]{:S(2)}) async-start(), calls=%async_computation.19 | async-start | bytes 524288 | tf_op jit(solution)/shard_map/psum | solution.py:61
  283.8 129.1 %all-to-all-start.6 = ((f32[128,4,64]{0,2,1:T(8,128)}), f32[128,4,64]{0,2,1:T(8,128)S(1)}, u32[]{:S(2)}, u32[]{:S(2)}) async-start(f32[128,4,64]{0,2,1:T(8,128)} %bitcast.28), calls=%async_computation.7 | async-start | bytes 262144 | tf_op jit(solution)/shard_map/all_to_all | solution.py:85
  424.9 25.5 %all-to-all-start.7 = ((bf16[4,512,64]{1,2,0:T(8,128)(2,1)}), bf16[4,512,64]{1,2,0:T(8,128)(2,1)S(1)}, u32[]{:S(2)}, u32[]{:S(2)}) async-start(bf16[4,512,64]{1,2,0:T(8,128)(2,1)} %copy.192), calls=%async_computation.8 | async-start | bytes 524288 | tf_op jit(solution)/shard_map/all_to_all | solution.py:31
  455.2 20.0 %all-to-all-start.8 = ((f32[1,512,256]{1,0,2:T(1,128)}), f32[1,512,256]{1,0,2:T(1,128)S(1)}, u32[]{:S(2)}, u32[]{:S(2)}) async-start(f32[1,512,256]{1,0,2:T(1,128)} %copy.193), calls=%async_computation.9 | async-start | bytes 1048576 | tf_op jit(solution)/shard_map/all_to_all | solution.py:44
  460.3 54.2 %reduce-scatter.5.cloned.1.call-start = ((), (), s32[]{:S(2)}) async-start(), calls=%async_computation.18 | async-start | bytes 1179648 | tf_op jit(solution)/shard_map/reduce_scatter | solution.py:51
  516.1 10.5 %all-to-all-start.9 = ((f32[4,128,64]{1,2,0:T(8,128)}), f32[4,128,64]{1,2,0:T(8,128)S(1)}, u32[]{:S(2)}, u32[]{:S(2)}) async-start(f32[4,128,64]{1,2,0:T(8,128)} %copy_bitcast_fusion.5), calls=%async_computation.11 | async-start | bytes 262144 | tf_op jit(solution)/shard_map/all_to_all | solution.py:76
  526.6 9.2 %all-to-all-start.12 = ((f32[128,4,64]{0,2,1:T(8,128)}), f32[128,4,64]{0,2,1:T(8,128)S(1)}, u32[]{:S(2)}, u32[]{:S(2)}) async-start(f32[128,4,64]{0,2,1:T(8,128)} %bitcast.54), calls=%async_computation.14 | async-start | bytes 262144 | tf_op jit(solution)/shard_map/all_to_all | solution.py:86
  535.9 9.2 %all-to-all-start.11 = ((f32[128,4,64]{0,2,1:T(8,128)}), f32[128,4,64]{0,2,1:T(8,128)S(1)}, u32[]{:S(2)}, u32[]{:S(2)}) async-start(f32[128,4,64]{0,2,1:T(8,128)} %bitcast.52), calls=%async_computation.13 | async-start | bytes 262144 | tf_op jit(solution)/shard_map/all_to_all | solution.py:85
  545.1 9.2 %all-to-all-start.13 = ((f32[128,4,64]{0,2,1:T(8,128)}), f32[128,4,64]{0,2,1:T(8,128)S(1)}, u32[]{:S(2)}, u32[]{:S(2)}) async-start(f32[128,4,64]{0,2,1:T(8,128)} %bitcast.56), calls=%async_computation.15 | async-start | bytes 262144 | tf_op jit(solution)/shard_map/all_to_all | solution.py:86
Sparse Core Ops, SparseCore 0:
  44.9 128.9 all-reduce.3
  283.4 127.0 all-reduce.5
Sparse Core Ops, SparseCore 1:
  224.3 37.3 reduce-scatter.2
  477.9 36.6 reduce-scatter.4
where the time goes:
time: 572 us; the launch traced here: 563 us
  waiting for transfers between devices  302 us (53%)
  other arithmetic  113 us (20%)
  starting transfers between devices  57 us (10%)
  local copies, waits for them, and re-layouts  30.9 us (5%)
  between operations  20.2 us (4%)
  blocking collectives  19.8 us (3%)
  matrix products  19.7 us (3%)
    psum x2, waiting for transfers between devices, joint_gram(): total = lax.psum(local_gram, ('wide', 'narrow'))  239 us
    another operation x13, other arithmetic, joint_gram(): lower = jnp.linalg.cholesky(gram + penalty * identity)  68.5 us
    another operation x5, other arithmetic, joint_gram(): inverse = jax.scipy.linalg.cho_solve((lower, True), identity)  39.4 us
    reduce_scatter x2, waiting for transfers between devices, owner_sums(): lax.psum_scatter(placed.reshape(owned * lax.axis_size('wide'), width), 'w...  23.4 us
    all_gather x2, blocking collectives, fetch_rows(): portion = lax.all_gather(lowered, 'wide', axis=0, tiled=True)  19.8 us
  transfers between devices with their start and end apart: 18, of which 12 were waited for; matrix products, arithmetic and copies ran while one was open for 25% of the time, Pallas kernels for 0%

commit v1 on v0

--- a/solution.py
+++ b/solution.py
@@ -58,7 +58,9 @@
 
 def joint_gram(other_rows, time_factor):
     local_gram = jnp.dot(other_rows.T, other_rows, precision=lax.Precision.HIGHEST)
-    total = lax.psum(local_gram, ("wide", "narrow"))
+    total = local_gram
+    for axis in ("wide", "narrow"):
+        total = lax.psum(total, axis)
     gram = total * jnp.dot(time_factor.T, time_factor, precision=lax.Precision.HIGHEST)
     penalty = jnp.trace(gram) / RANK
     identity = jnp.eye(RANK, dtype=jnp.float32)

time: 572 us -> 494 us (0.86)
  waiting for transfers between devices: 302 us -> 231 us
    psum x2 -> x4, waiting for transfers between devices: 239 us -> 167 us  [joint_gram(): total = lax.psum(total, axis)]
  transfers between devices with their start and end apart: 18 -> 20, of which waited for: 12 -> 14; matrix products, arithmetic and copies ran while one was open for 25% -> 30% of each run, Pallas kernels for 0% -> 0%
where the time goes in v1:
time: 494 us; the launch traced here: 489 us
  waiting for transfers between devices  231 us (47%)
  other arithmetic  113 us (23%)
  starting transfers between devices  57.6 us (12%)
  local copies, waits for them, and re-layouts  29.3 us (6%)
  matrix products  19.7 us (4%)
  blocking collectives  19 us (4%)
  between operations  18.9 us (4%)
    psum x4, waiting for transfers between devices, joint_gram(): total = lax.psum(total, axis)  167 us
    another operation x13, other arithmetic, joint_gram(): lower = jnp.linalg.cholesky(gram + penalty * identity)  68.7 us
    another operation x5, other arithmetic, joint_gram(): inverse = jax.scipy.linalg.cho_solve((lower, True), identity)  39.4 us
    reduce_scatter x2, waiting for transfers between devices, owner_sums(): lax.psum_scatter(placed.reshape(owned * lax.axis_size('wide'), width), 'w...  23.5 us
    all_gather x2, blocking collectives, fetch_rows(): portion = lax.all_gather(lowered, 'wide', axis=0, tiled=True)  19 us
    all_to_all x2, waiting for transfers between devices, update_rows(): lax.all_to_all(sums, 'narrow', split_axis=0, concat_axis=1, tiled=True)  11.3 us
  transfers between devices with their start and end apart: 20, of which 14 were waited for; matrix products, arithmetic and copies ran while one was open for 30% of the time, Pallas kernels for 0%

profile of v1, /device:TPU:0, one launch (start us, length us, event | category | flops | bytes accessed | tf_op | source)
XLA Modules:
  0.0 489.0 jit_solution(4375187541683312818)
XLA Ops:
  7.2 1.6 copy_bitcast_fusion.8
  8.8 6.3 %all-to-all-start.3 = ((f32[4,128,64]{1,2,0:T(8,128)}), f32[4,128,64]{1,2,0:T(8,128)S(1)}, u32[]{:S(2)}, u32[]{:S(2)}) async-start(f32[4,128,64]{1,2,0:T(8,128)} %copy_bitcast_fusion.8), calls=%async_computation.4 | async-start | bytes 262144 | tf_op jit(solution)/shard_map/all_to_all | solution.py:113
  15.2 0.9 convert_element_type.70
  16.1 9.9 %all_gather.6 = bf16[4096,64]{0,1:T(8,128)(2,1)S(1)} all-gather(bf16[512,64]{0,1:T(8,128)(2,1)S(1)} %convert_element_type.70), channel_id=1, replica_groups=mesh['wide'=8,'narrow'=4] {'wide'}, dimensions={0}, use_global_device_ids=true | all-gather | bytes 589824 | tf_op jit(solution)/shard_map/all_gather | solution.py:22
  26.9 0.8 select_reduce_fusion.6
  28.9 0.8 select_reduce_fusion.7
  30.4 5.1 %all-to-all-start.4 = ((f32[4,128,64]{1,2,0:T(8,128)}), f32[4,128,64]{1,2,0:T(8,128)S(1)}, u32[]{:S(2)}, u32[]{:S(2)}) async-start(f32[4,128,64]{1,2,0:T(8,128)} %copy_bitcast_fusion.7), calls=%async_computation.5 | async-start | bytes 262144 | tf_op jit(solution)/shard_map/all_to_all | solution.py:111
  36.1 5.8 %all-to-all-done.4 = f32[4,128,64]{1,2,0:T(8,128)S(1)} async-done(((f32[4,128,64]{1,2,0:T(8,128)}), f32[4,128,64]{1,2,0:T(8,128)S(1)}, u32[]{:S(2)}, u32[]{:S(2)}) %all-to-all-start.4) | async-done | bytes 131104 | tf_op jit(solution)/shard_map/all_to_all | solution.py:111
  41.9 3.3 all-to-all-start.5
  45.9 5.2 %all-to-all-done.5 = f32[4,128,64]{1,2,0:T(8,128)S(1)} async-done(((f32[4,128,64]{1,2,0:T(8,128)}), f32[4,128,64]{1,2,0:T(8,128)S(1)}, u32[]{:S(2)}, u32[]{:S(2)}) %all-to-all-start.5) | async-done | bytes 131104 | tf_op jit(solution)/shard_map/all_to_all | solution.py:112
  51.1 3.4 all-to-all-start
  54.6 1.1 fusion.86
  56.0 56.8 %all-reduce.6.cloned.1.call-done = f32[256,256]{0,1:T(8,128)} async-done(((f32[256,256]{0,1:T(8,128)}), f32[256,256]{0,1:T(8,128)}) %all-reduce.6.cloned.1.call-update) | async-done | bytes 262160 | tf_op jit(solution)/shard_map/psum | solution.py:63
  112.8 3.5 fusion.8
  116.3 1.3 copy.174
  117.6 4.6 all-to-all-start.1
  122.5 32.8 %all-reduce.8.cloned.1.call-done = f32[256,256]{0,1:T(8,128)} async-done(((f32[256,256]{0,1:T(8,128)}), f32[256,256]{0,1:T(8,128)}) %all-reduce.8.cloned.1.call-update) | async-done | bytes 262160 | tf_op jit(solution)/shard_map/psum | solution.py:63
  155.3 2.0 select_reduce_fusion.1
  158.2 11.7 %cholesky.130 = f32[128,128]{1,0:T(8,128)S(1)} custom-call(f32[128,128]{1,0:T(8,128)S(1)} %cholesky.194), custom_call_target="Cholesky" | custom-call | tf_op jit(solution)/shard_map/jit(cholesky)/cholesky | solution.py:67
  169.9 9.8 %custom-call.15 = f32[1,128,128]{1,2,0:T(8,128)S(1)} custom-call(f32[1,128,128]{2,1,0:T(8,128)S(1)} %get-tuple-element.59), custom_call_target="InvertDiagBlocksLowerTriangular" | custom-call | tf_op jit(solution)/shard_map/jit(cholesky)/cholesky | solution.py:67
  180.2 11.7 %cholesky.147 = f32[128,128]{1,0:T(8,128)S(1)} custom-call(f32[128,128]{1,0:T(8,128)S(1)} %convolution_subtract_fusion.5), custom_call_target="Cholesky" | custom-call | tf_op jit(solution)/shard_map/jit(cholesky)/cholesky | solution.py:67
  194.1 1.0 fusion.16
  195.2 2.1 copy.231
  197.4 3.8 while.4
  198.0 1.3 bitcast_dynamic-update-slice_fusion.4
  199.9 1.3 bitcast_dynamic-update-slice_fusion.4
  201.2 19.7 %custom-call.16 = f32[2,128,128]{1,2,0:T(8,128)S(1)} custom-call(f32[2,128,128]{2,1,0:T(8,128)S(1)} %get-tuple-element.20), custom_call_target="InvertDiagBlocksLowerTriangular" | custom-call | tf_op jit(solution)/shard_map/jit(_cho_solve)/triangular_solve | solution.py:68
  222.5 11.0 %reduce-scatter.3.cloned.1.call-done = f32[512,64]{0,1:T(8,128)} async-done(((f32[4096,64]{0,1:T(8,128)}), f32[512,64]{0,1:T(8,128)}) %reduce-scatter.3.cloned.1.call-update) | async-done | bytes 131088 | tf_op jit(solution)/shard_map/reduce_scatter | solution.py:51
  233.5 1.6 copy_bitcast_fusion.9
  235.0 4.6 all-to-all-start.2
  239.9 5.7 %all-to-all-done.2 = f32[4,128,64]{1,2,0:T(8,128)S(1)} async-done(((f32[4,128,64]{1,2,0:T(8,128)}), f32[4,128,64]{1,2,0:T(8,128)S(1)}, u32[]{:S(2)}, u32[]{:S(2)}) %all-to-all-start.2) | async-done | bytes 131104 | tf_op jit(solution)/shard_map/all_to_all | solution.py:78
  245.5 3.3 all-to-all-start.10
  250.4 4.4 all-to-all-done.10
  254.8 3.3 all-to-all-start.6
  258.1 1.1 fusion.87
  259.5 0.8 copy.209
  260.3 55.7 %all-reduce.10.cloned.1.call-done = f32[256,256]{0,1:T(8,128)} async-done(((f32[256,256]{0,1:T(8,128)}), f32[256,256]{0,1:T(8,128)}) %all-reduce.10.cloned.1.call-update) | async-done | bytes 262160 | tf_op jit(solution)/shard_map/psum | solution.py:63
  316.7 9.2 %all_gather.7 = bf16[4096,64]{0,1:T(8,128)(2,1)S(1)} all-gather(bf16[512,64]{0,1:T(8,128)(2,1)S(1)} %get-tuple-element.40), channel_id=1, replica_groups=mesh['wide'=8,'narrow'=4] {'wide'}, dimensions={0}, use_global_device_ids=true | all-gather | bytes 589824 | tf_op jit(solution)/shard_map/all_gather | solution.py:22
  327.2 4.8 all-to-all-start.7
  331.9 21.5 %all-reduce.12.cloned.1.call-done = f32[256,256]{0,1:T(8,128)} async-done(((f32[256,256]{0,1:T(8,128)}), f32[256,256]{0,1:T(8,128)}) %all-reduce.12.cloned.1.call-update) | async-done | bytes 262160 | tf_op jit(solution)/shard_map/psum | solution.py:63
  353.5 1.6 select_reduce_fusion
  356.0 11.7 %cholesky.164 = f32[128,128]{1,0:T(8,128)S(1)} custom-call(f32[128,128]{1,0:T(8,128)S(1)} %cholesky.197), custom_call_target="Cholesky" | custom-call | tf_op jit(solution)/shard_map/jit(cholesky)/cholesky | solution.py:67
  367.7 9.8 %custom-call.17 = f32[1,128,128]{1,2,0:T(8,128)S(1)} custom-call(f32[1,128,128]{2,1,0:T(8,128)S(1)} %get-tuple-element.55), custom_call_target="InvertDiagBlocksLowerTriangular" | custom-call | tf_op jit(solution)/shard_map/jit(cholesky)/cholesky | solution.py:67
  377.8 3.5 fusion.11
  381.3 1.3 copy.193
  382.7 3.5 all-to-all-start.8
  386.7 11.7 %cholesky.181 = f32[128,128]{1,0:T(8,128)S(1)} custom-call(f32[128,128]{1,0:T(8,128)S(1)} %convolution_subtract_fusion.4), custom_call_target="Cholesky" | custom-call | tf_op jit(solution)/shard_map/jit(cholesky)/cholesky | solution.py:67
  401.2 1.0 fusion.14
  402.2 1.6 copy.233
  403.8 3.8 while.5
  404.5 1.3 bitcast_dynamic-update-slice_fusion.5
  406.4 1.3 bitcast_dynamic-update-slice_fusion.5
  407.7 19.7 %custom-call.18 = f32[2,128,128]{1,2,0:T(8,128)S(1)} custom-call(f32[2,128,128]{2,1,0:T(8,128)S(1)} %get-tuple-element.21), custom_call_target="InvertDiagBlocksLowerTriangular" | custom-call | tf_op jit(solution)/shard_map/jit(_cho_solve)/triangular_solve | solution.py:68
  429.0 12.5 %reduce-scatter.5.cloned.1.call-done = f32[512,64]{0,1:T(8,128)} async-done(((f32[4096,64]{0,1:T(8,128)}), f32[512,64]{0,1:T(8,128)}) %reduce-scatter.5.cloned.1.call-update) | async-done | bytes 131088 | tf_op jit(solution)/shard_map/reduce_scatter | solution.py:51
  441.5 1.6 copy_bitcast_fusion.5
  443.0 4.6 all-to-all-start.9
  447.9 5.7 %all-to-all-done.9 = f32[4,128,64]{1,2,0:T(8,128)S(1)} async-done(((f32[4,128,64]{1,2,0:T(8,128)}), f32[4,128,64]{1,2,0:T(8,128)S(1)}, u32[]{:S(2)}, u32[]{:S(2)}) %all-to-all-start.9) | async-done | bytes 131104 | tf_op jit(solution)/shard_map/all_to_all | solution.py:78
  453.6 3.3 all-to-all-start.12
  457.6 0.8 copy.207
  458.4 4.4 all-to-all-done.12
  462.8 3.3 all-to-all-start.11
  467.5 4.5 all-to-all-done.11
  472.0 3.3 all-to-all-start.13
  476.0 5.2 %all-to-all-done.13 = f32[128,4,64]{0,2,1:T(8,128)S(1)} async-done(((f32[128,4,64]{0,2,1:T(8,128)}), f32[128,4,64]{0,2,1:T(8,128)S(1)}, u32[]{:S(2)}, u32[]{:S(2)}) %all-to-all-start.13) | async-done | bytes 131104 | tf_op jit(solution)/shard_map/all_to_all | solution.py:88
  (105 shorter events, 22.0 us)
Async XLA Ops:
  7.2 22.5 %copy-start = (f32[512,64]{0,1:T(8,128)S(1)}, f32[512,64]{0,1:T(8,128)}, u32[]{:S(2)}) copy-start(f32[512,64]{0,1:T(8,128)} %param.16) | copy-start | bytes 393220
  7.2 28.3 %copy-start.1 = (f32[512,64]{0,1:T(8,128)S(1)}, f32[512,64]{0,1:T(8,128)}, u32[]{:S(2)}) copy-start(f32[512,64]{0,1:T(8,128)} %param.19) | copy-start | bytes 393220
  7.2 38.0 %copy-start.2 = (f32[512,64]{0,1:T(8,128)S(1)}, f32[512,64]{0,1:T(8,128)}, u32[]{:S(2)}) copy-start(f32[512,64]{0,1:T(8,128)} %param.20) | copy-start | bytes 393220
  7.2 105.6 %copy-start.3 = (f32[8,256]{1,0:T(8,128)S(1)}, f32[8,256]{1,0:T(8,128)}, u32[]{:S(2)}) copy-start(f32[8,256]{1,0:T(8,128)} %param.18) | copy-start | bytes 24580
  8.8 21.5 %all-to-all-start.3 = ((f32[4,128,64]{1,2,0:T(8,128)}), f32[4,128,64]{1,2,0:T(8,128)S(1)}, u32[]{:S(2)}, u32[]{:S(2)}) async-start(f32[4,128,64]{1,2,0:T(8,128)} %copy_bitcast_fusion.8), calls=%async_computation.4 | async-start | bytes 262144 | tf_op jit(solution)/shard_map/all_to_all | solution.py:113
  30.4 11.5 %all-to-all-start.4 = ((f32[4,128,64]{1,2,0:T(8,128)}), f32[4,128,64]{1,2,0:T(8,128)S(1)}, u32[]{:S(2)}, u32[]{:S(2)}) async-start(f32[4,128,64]{1,2,0:T(8,128)} %copy_bitcast_fusion.7), calls=%async_computation.5 | async-start | bytes 262144 | tf_op jit(solution)/shard_map/all_to_all | solution.py:111
  41.9 9.2 %all-to-all-start.5 = ((f32[4,128,64]{1,2,0:T(8,128)}), f32[4,128,64]{1,2,0:T(8,128)S(1)}, u32[]{:S(2)}, u32[]{:S(2)}) async-start(f32[4,128,64]{1,2,0:T(8,128)} %copy_bitcast_fusion.6), calls=%async_computation.6 | async-start | bytes 262144 | tf_op jit(solution)/shard_map/all_to_all | solution.py:112
  51.1 61.7 %all-to-all-start = ((bf16[4,512,64]{1,2,0:T(8,128)(2,1)}), bf16[4,512,64]{1,2,0:T(8,128)(2,1)S(1)}, u32[]{:S(2)}, u32[]{:S(2)}) async-start(bf16[4,512,64]{1,2,0:T(8,128)(2,1)} %copy.173), calls=%async_computation | async-start | bytes 524288 | tf_op jit(solution)/shard_map/all_to_all | solution.py:31
  54.5 58.2 %all-reduce.6.cloned.1.call-start = ((), (), s32[]{:S(2)}) async-start(), calls=%async_computation.17 | async-start | bytes 524288 | tf_op jit(solution)/shard_map/psum | solution.py:63
  55.7 99.6 %all-reduce.8.cloned.1.call-start = ((), (), s32[]{:S(2)}) async-start(), calls=%async_computation.18 | async-start | bytes 524288 | tf_op jit(solution)/shard_map/psum | solution.py:63
  117.6 76.4 %all-to-all-start.1 = ((f32[1,512,256]{1,0,2:T(1,128)}), f32[1,512,256]{1,0,2:T(1,128)S(1)}, u32[]{:S(2)}, u32[]{:S(2)}) async-start(f32[1,512,256]{1,0,2:T(1,128)} %copy.174), calls=%async_computation.1 | async-start | bytes 1048576 | tf_op jit(solution)/shard_map/all_to_all | solution.py:44
  122.2 111.2 %reduce-scatter.3.cloned.1.call-start = ((), (), s32[]{:S(2)}) async-start(), calls=%async_computation.16 | async-start | bytes 1179648 | tf_op jit(solution)/shard_map/reduce_scatter | solution.py:51
  235.0 10.5 %all-to-all-start.2 = ((f32[4,128,64]{1,2,0:T(8,128)}), f32[4,128,64]{1,2,0:T(8,128)S(1)}, u32[]{:S(2)}, u32[]{:S(2)}) async-start(f32[4,128,64]{1,2,0:T(8,128)} %copy_bitcast_fusion.9), calls=%async_computation.3 | async-start | bytes 262144 | tf_op jit(solution)/shard_map/all_to_all | solution.py:78
  245.5 9.2 %all-to-all-start.10 = ((f32[4,128,64]{1,2,0:T(8,128)}), f32[4,128,64]{1,2,0:T(8,128)S(1)}, u32[]{:S(2)}, u32[]{:S(2)}) async-start(f32[4,128,64]{1,2,0:T(8,128)} %copy_bitcast_fusion.4), calls=%async_computation.12 | async-start | bytes 262144 | tf_op jit(solution)/shard_map/all_to_all | solution.py:114
  254.8 61.3 %all-to-all-start.6 = ((f32[128,4,64]{0,2,1:T(8,128)}), f32[128,4,64]{0,2,1:T(8,128)S(1)}, u32[]{:S(2)}, u32[]{:S(2)}) async-start(f32[128,4,64]{0,2,1:T(8,128)} %bitcast.28), calls=%async_computation.7 | async-start | bytes 262144 | tf_op jit(solution)/shard_map/all_to_all | solution.py:87
  258.1 57.9 %all-reduce.10.cloned.1.call-start = ((), (), s32[]{:S(2)}) async-start(), calls=%async_computation.20 | async-start | bytes 524288 | tf_op jit(solution)/shard_map/psum | solution.py:63
  259.3 94.2 %all-reduce.12.cloned.1.call-start = ((), (), s32[]{:S(2)}) async-start(), calls=%async_computation.21 | async-start | bytes 524288 | tf_op jit(solution)/shard_map/psum | solution.py:63
  327.2 50.6 %all-to-all-start.7 = ((bf16[4,512,64]{1,2,0:T(8,128)(2,1)}), bf16[4,512,64]{1,2,0:T(8,128)(2,1)S(1)}, u32[]{:S(2)}, u32[]{:S(2)}) async-start(bf16[4,512,64]{1,2,0:T(8,128)(2,1)} %copy.192), calls=%async_computation.8 | async-start | bytes 524288 | tf_op jit(solution)/shard_map/all_to_all | solution.py:31
  382.7 18.5 %all-to-all-start.8 = ((f32[1,512,256]{1,0,2:T(1,128)}), f32[1,512,256]{1,0,2:T(1,128)S(1)}, u32[]{:S(2)}, u32[]{:S(2)}) async-start(f32[1,512,256]{1,0,2:T(1,128)} %copy.193), calls=%async_computation.9 | async-start | bytes 1048576 | tf_op jit(solution)/shard_map/all_to_all | solution.py:44
  386.2 55.3 %reduce-scatter.5.cloned.1.call-start = ((), (), s32[]{:S(2)}) async-start(), calls=%async_computation.19 | async-start | bytes 1179648 | tf_op jit(solution)/shard_map/reduce_scatter | solution.py:51
  443.0 10.5 %all-to-all-start.9 = ((f32[4,128,64]{1,2,0:T(8,128)}), f32[4,128,64]{1,2,0:T(8,128)S(1)}, u32[]{:S(2)}, u32[]{:S(2)}) async-start(f32[4,128,64]{1,2,0:T(8,128)} %copy_bitcast_fusion.5), calls=%async_computation.11 | async-start | bytes 262144 | tf_op jit(solution)/shard_map/all_to_all | solution.py:78
  453.6 9.2 %all-to-all-start.12 = ((f32[128,4,64]{0,2,1:T(8,128)}), f32[128,4,64]{0,2,1:T(8,128)S(1)}, u32[]{:S(2)}, u32[]{:S(2)}) async-start(f32[128,4,64]{0,2,1:T(8,128)} %bitcast.54), calls=%async_computation.14 | async-start | bytes 262144 | tf_op jit(solution)/shard_map/all_to_all | solution.py:88
  462.8 9.2 %all-to-all-start.11 = ((f32[128,4,64]{0,2,1:T(8,128)}), f32[128,4,64]{0,2,1:T(8,128)S(1)}, u32[]{:S(2)}, u32[]{:S(2)}) async-start(f32[128,4,64]{0,2,1:T(8,128)} %bitcast.52), calls=%async_computation.13 | async-start | bytes 262144 | tf_op jit(solution)/shard_map/all_to_all | solution.py:87
  472.0 9.2 %all-to-all-start.13 = ((f32[128,4,64]{0,2,1:T(8,128)}), f32[128,4,64]{0,2,1:T(8,128)S(1)}, u32[]{:S(2)}, u32[]{:S(2)}) async-start(f32[128,4,64]{0,2,1:T(8,128)} %bitcast.56), calls=%async_computation.15 | async-start | bytes 262144 | tf_op jit(solution)/shard_map/all_to_all | solution.py:88
Sparse Core Ops, SparseCore 0:
  58.4 54.3 all-reduce.5
  115.1 40.2 all-reduce.7
  197.4 36.0 reduce-scatter.2
  261.7 54.3 all-reduce.9
  318.2 35.2 all-reduce.11
  404.0 37.4 reduce-scatter.4
